TPU v7x, 256 devices: a whole 4x4x8 slice. The times are simulated.
256 devices in a mesh: seq: 64 (over z, x, y_lo), head: 4 (over y_hi, core).
Axes of the slice: x: 4, y: 4 (y_hi: 2, y_lo: 2; y = y_hi * 2 + y_lo), z: 8, core: 2. Of those that a mesh axis runs over, the one named last changes fastest.
Arguments:
- query: bfloat16 [8192, 3072], P('seq', 'head'), may hold values from -256 to 256
- keys: bfloat16 [8192, 3072], P('seq', 'head'), may hold values from -4 to 4
- values: bfloat16 [8192, 3072], P('seq', 'head'), may hold values from -5 to 5
- out_weight: bfloat16 [3072, 4096], P('head'), may hold values from -0.109375 to 0.109375
- image_start: int32 [3], replicated, may hold values from 0 to 7168, as said below
Outputs:
- mixed: bfloat16 [8192, 4096], P('seq', 'head')
Inputs may be any that keep to these rules, and one draw needn't show every extreme that they name: `image_start`: the starts increase; each image's 1024 positions lie inside the sequence and no two images share a position; the last image ends at the sequence's end.
All inputs are finite; a program needn't handle non-finite values.
Results may differ from a plain program's by a relative error of at most 0.012.
Values may be sent and summed in bfloat16 or wider, within the bound.
A program may use at most 192 MiB of HBM per device.

v0:
```python
import jax
import jax.numpy as jnp
from jax import lax
from jax.sharding import PartitionSpec as P

HEAD_DIM = 128


def image_tags(positions, image_start, patch_count):
    inside = (positions[:, None] >= image_start[None, :]) & (
        positions[:, None] < image_start[None, :] + patch_count
    )
    labels = jnp.arange(image_start.shape[0], dtype=jnp.int32) + 1
    return jnp.sum(jnp.where(inside, labels[None, :], 0), axis=1) - 1


def body(query, keys, values, out_weight, image_start):
    cycle_size = lax.axis_size("seq")
    own_index = lax.axis_index("seq")
    row_count = query.shape[0]
    seq_total = row_count * cycle_size
    patch_count = min(1024, seq_total // 8)
    head_count = query.shape[1] // HEAD_DIM
    scale = HEAD_DIM ** (-0.5)
    query_pos = own_index * row_count + jnp.arange(row_count, dtype=jnp.int32)
    query_heads = jnp.transpose(query.reshape(row_count, head_count, HEAD_DIM), (1, 0, 2))
    query_tag = image_tags(query_pos, image_start, patch_count)
    initial = (
        jnp.full((head_count, row_count), -1e30, jnp.float32),
        jnp.zeros((head_count, row_count), jnp.float32),
        jnp.zeros((head_count, row_count, HEAD_DIM), jnp.float32),
    )
    key_major = jnp.transpose(keys.reshape(row_count, head_count, HEAD_DIM), (1, 0, 2))
    value_major = jnp.transpose(values.reshape(row_count, head_count, HEAD_DIM), (1, 0, 2))
    key_value = jnp.stack((key_major, value_major))
    block_pair = lax.all_gather(key_value, "seq", axis=2, tiled=True)
    piece_len = block_pair.shape[2]
    key_pos = jnp.arange(piece_len, dtype=jnp.int32)
    key_tag = image_tags(key_pos, image_start, patch_count)
    in_range = (key_pos >= 0) & (key_pos < seq_total)
    visible = in_range[None, :] & (
        (key_pos[None, :] <= query_pos[:, None])
        | (query_tag[:, None] == key_tag[None, :]) & (query_tag[:, None] >= 0)
    )

    def compute(state_old):
        row_high, row_sum, weighted = state_old
        key_block = block_pair[0]
        value_block = block_pair[1]
        scores = (
            jnp.einsum("hqd,hkd->hqk", query_heads, key_block, preferred_element_type=jnp.float32)
            * scale
        )
        scores = jnp.where(visible[None], scores, -1e30)
        new_high = jnp.maximum(row_high, jnp.max(scores, axis=-1))
        weights = jnp.where(visible[None], jnp.exp(scores - new_high[..., None]), 0.0)
        row_sum = jnp.sum(weights, axis=-1)
        update = jnp.einsum(
            "hqk,hkd->hqd",
            weights.astype(jnp.bfloat16),
            value_block,
            preferred_element_type=jnp.float32,
        )
        weighted = update
        return (new_high, row_sum, weighted)

    def unchanged(state_old):
        return state_old

    state_now = lax.cond(jnp.any(visible), compute, unchanged, initial)
    row_high, row_sum, weighted = state_now
    attended = (weighted / row_sum[..., None]).astype(jnp.bfloat16)
    attended_rows = jnp.transpose(attended, (1, 0, 2)).reshape(row_count, head_count * HEAD_DIM)
    partial_value = jnp.dot(attended_rows, out_weight, preferred_element_type=jnp.float32)
    return lax.psum_scatter(
        partial_value.astype(jnp.bfloat16), "head", scatter_dimension=1, tiled=True
    )


def solution(mesh):
    placed = (P("seq", "head"), P("seq", "head"), P("seq", "head"), P("head", None), P())
    return jax.shard_map(
        body, mesh=mesh, in_specs=placed, out_specs=P("seq", "head"), check_vma=False
    )
```

profile of v0, /device:TPU:1, one launch (start us, length us, event | category | flops | bytes accessed | tf_op | source)
XLA Modules:
  0.0 784.2 jit_solution(2414290603275093940)
XLA Ops:
  6.5 0.0 all-gather.2.cloned.1.call-start
  6.5 1.1 copy.12
  7.6 1.1 copy.13
  8.7 0.8 pad_maximum_fusion
  9.6 0.0 all-gather.2.cloned.1.call-update
  9.6 0.0 reduce-scatter.2.cloned.1.call-start
  9.6 1.1 copy.14
  10.8 0.7 iota_add_fusion
  11.4 0.7 select_reduce_fusion.1
  12.2 0.8 select_reduce_fusion
  13.0 2.6 fusion.16
  16.3 603.2 %all-gather.2.cloned.1.call-done = bf16[2,6,8192,128]{2,3,1,0:T(8,128)(2,1)} async-done(((bf16[2,6,128,128]{2,3,1,0:T(8,128)(2,1)}), bf16[2,6,8192,128]{2,3,1,0:T(8,128)(2,1)}) %all-gather.2.cloned.1.call-update) | async-done | bytes 25165840 | tf_op jit(solution)/shard_map/all_gather | solution.py:36
  619.5 74.4 %conditional.1 = (f32[6,128]{1,0:T(8,128)S(1)}, f32[6,128,128]{1,2,0:T(8,128)S(1)}) conditional(s32[]{:T(128)} %convert_element_type.12, () %tuple.13, (pred[128,8192]{1,0:T(8,128)(4,1)S(1)}, bf16[2,6,8192,128]{2,3,1,0:T(8,128)(2,1)}, bf16[6,128,128]{1,2,0:T(8,128)(2,1)S(1)}) %tuple.28), branch_computations={%region_3.4_spmd, %region_4.7_spmd} | conditional | flops 3303013632 | bytes 154748944 | solution.py:70
  619.5 32.6 %copy.15 = bf16[2,6,8192,128]{3,2,1,0:T(8,128)(2,1)} copy(bf16[2,6,8192,128]{2,3,1,0:T(8,128)(2,1)} %get-tuple-element.22) | data formatting | bytes 50331648 | tf_op jit(solution)/shard_map
  652.1 13.6 %fusion = (f32[6,128]{1,0:T(8,128)S(1)}, f32[6,128,8192]{2,1,0:T(8,128)}) fusion(pred[128,8192]{1,0:T(8,128)(4,1)S(1)} %get-tuple-element.11, bf16[6,128,128]{1,2,0:T(8,128)(2,1)S(1)} %get-tuple-element.23, bf16[2,6,8192,128]{3,2,1,0:T(8,128)(2,1)} %copy.15), kind=kOutput, calls=%fused_computation.2 | convolution fusion | flops 1629486336 | bytes 38996992 | tf_op jit(solution)/shard_map/cond/branch_1_fun/hqd,hkd->hqk/dot_general | solution.py:51
  665.7 15.8 %fusion.3 = f32[6,128,128]{1,2,0:T(8,128)S(1)} fusion(bf16[2,6,8192,128]{3,2,1,0:T(8,128)(2,1)} %copy.15, f32[6,128,8192]{2,1,0:T(8,128)} %get-tuple-element.28, f32[6,128]{1,0:T(8,128)S(1)} %broadcast_maximum_fusion, pred[128,8192]{1,0:T(8,128)(4,1)S(1)} %get-tuple-element.11), kind=kOutput, calls=%fused_computation.6 | convolution fusion | flops 1642070016 | bytes 39193600 | tf_op jit(solution)/shard_map/cond | solution.py:70
  681.4 12.5 %fusion.2 = f32[6,128]{1,0:T(8,128)S(1)} fusion(f32[6,128,8192]{2,1,0:T(8,128)} %get-tuple-element.28, f32[6,128]{1,0:T(8,128)S(1)} %broadcast_maximum_fusion, pred[128,8192]{1,0:T(8,128)(4,1)S(1)} %get-tuple-element.11), kind=kLoop, calls=%fused_computation.4 | loop fusion | flops 31456512 | bytes 26220544 | tf_op jit(solution)/shard_map/cond/branch_1_fun/reduce_sum | solution.py:57
  693.9 4.8 convolution_convert_fusion
  698.7 0.0 reduce-scatter.2.cloned.1.call-update
  698.8 78.6 %reduce-scatter.2.cloned.1.call-done = bf16[128,1024]{1,0:T(8,128)(2,1)} async-done(((bf16[128,4096]{1,0:T(8,128)(2,1)}), bf16[128,1024]{1,0:T(8,128)(2,1)}) %reduce-scatter.2.cloned.1.call-update) | async-done | bytes 262160 | tf_op jit(solution)/shard_map/reduce_scatter | solution.py:75
  (7 shorter events, 0.1 us)
Async XLA Ops:
  6.5 612.9 %all-gather.2.cloned.1.call-start = ((), (), s32[]{:S(2)}) async-start(), calls=%async_computation.1 | async-start | bytes 25559040 | tf_op jit(solution)/shard_map/all_gather | solution.py:36
  9.6 767.8 %reduce-scatter.2.cloned.1.call-start = ((), (), s32[]{:S(2)}) async-start(), calls=%async_computation.2 | async-start | bytes 1310720 | tf_op jit(solution)/shard_map/reduce_scatter | solution.py:75
Sparse Core Ops, SparseCore 0:
  9.7 609.7 all-gather.1
  698.9 78.4 reduce-scatter.1
where the time goes:
time: 785 us; the launch traced here: 784 us
  waiting for transfers between devices  682 us (87%)
  local copies, waits for them, and re-layouts  35.8 us (5%)
  matrix products  34.2 us (4%)
  other arithmetic  18.2 us (2%)
  between operations  14.1 us (2%)
    all_gather x1, waiting for transfers between devices, body(): block_pair = lax.all_gather(key_value, 'seq', axis=2, tiled=True)  603 us
    reduce_scatter x1, waiting for transfers between devices, body(): lax.psum_scatter(partial_value.astype(jnp.bfloat16), 'head', scatter_dime...  78.6 us
    another operation x1, local copies, waits for them, and re-layouts  32.6 us
    cond x1, matrix products, body(): state_now = lax.cond(jnp.any(visible), compute, unchanged, initial)  15.8 us
  transfers between devices with their start and end apart: 2, of which 2 were waited for; matrix products, arithmetic and copies ran while one was open for 1% of the time, Pallas kernels for 0%

commit v1 on v0

--- a/solution.py
+++ b/solution.py
@@ -33,7 +33,8 @@
     key_major = jnp.transpose(keys.reshape(row_count, head_count, HEAD_DIM), (1, 0, 2))
     value_major = jnp.transpose(values.reshape(row_count, head_count, HEAD_DIM), (1, 0, 2))
     key_value = jnp.stack((key_major, value_major))
-    block_pair = lax.all_gather(key_value, "seq", axis=2, tiled=True)
+    sent = jnp.stack([key_value] * lax.axis_size("seq"))
+    block_pair = jnp.concatenate(lax.all_to_all(sent, "seq", 0, 0), axis=2)
     piece_len = block_pair.shape[2]
     key_pos = jnp.arange(piece_len, dtype=jnp.int32)
     key_tag = image_tags(key_pos, image_start, patch_count)

time: 785 us -> 756 us (0.963)
  waiting for transfers between devices: 682 us -> 649 us
  starting transfers between devices: 0.04 us -> 13.9 us
    all_gather x1 -> x0, waiting for transfers between devices: 603 us -> none  [body(): block_pair = lax.all_gather(key_value, 'seq', axis=2, tiled=True)]
    all_to_all x0 -> x1, waiting for transfers between devices: none -> 582 us  [body(): block_pair = jnp.concatenate(lax.all_to_all(sent, 'seq', 0, 0), axis=2)]
    another operation x1 -> x2, local copies, waits for them, and re-layouts: 32.6 us -> 9.28 us  [the longest x1 9.05 us: body(): sent = jnp.stack([key_value] * lax.axis_size('seq'))]
    slice x0 -> x1, local copies, waits for them, and re-layouts: none -> 17.8 us  [compute(): value_block = block_pair[1]]
    all_to_all x0 -> x1, starting transfers between devices: none -> 13.8 us  [body(): block_pair = jnp.concatenate(lax.all_to_all(sent, 'seq', 0, 0), axis=2)]
    reduce_scatter x1, waiting for transfers between devices: 78.6 us -> 67 us  [body(): lax.psum_scatter(partial_value.astype(jnp.bfloat16), 'head', scatter_dime...]
  transfers between devices with their start and end apart: 2 -> 2, of which waited for: 2 -> 2; matrix products, arithmetic and copies ran while one was open for 1% -> 0% of each run, Pallas kernels for 0% -> 0%
where the time goes in v1:
time: 756 us
  waiting for transfers between devices  649 us (86%)
  matrix products  34.1 us (5%)
  local copies, waits for them, and re-layouts  29.4 us (4%)
  other arithmetic  15.4 us (2%)
  between operations  14.2 us (2%)
  starting transfers between devices  13.9 us (2%)
    all_to_all x1, waiting for transfers between devices, body(): block_pair = jnp.concatenate(lax.all_to_all(sent, 'seq', 0, 0), axis=2)  582 us
    reduce_scatter x1, waiting for transfers between devices, body(): lax.psum_scatter(partial_value.astype(jnp.bfloat16), 'head', scatter_dime...  67 us
    slice x1, local copies, waits for them, and re-layouts, compute(): value_block = block_pair[1]  17.8 us
    cond x1, matrix products, body(): state_now = lax.cond(jnp.any(visible), compute, unchanged, initial)  15.8 us
  transfers between devices with their start and end apart: 2, of which 2 were waited for; matrix products, arithmetic and copies ran while one was open for 0% of the time, Pallas kernels for 0%

profile of v1, /device:TPU:1, one launch (start us, length us, event | category | flops | bytes accessed | tf_op | source)
XLA Modules:
  0.0 755.8 jit_solution(1255880501721343532)
XLA Ops:
  6.5 1.1 copy.21
  7.6 1.1 copy.22
  8.8 0.2 copy.23
  9.0 9.1 %stack.11 = bf16[64,2,6,128,128]{4,3,2,1,0:T(8,128)(2,1)} broadcast(bf16[2,6,128,128]{3,2,1,0:T(8,128)(2,1)S(1)} %copy.23), dimensions={1,2,3,4} | broadcast | bytes 25559040 | tf_op jit(solution)/shard_map/stack | solution.py:36
  18.1 0.0 copy-start
  18.1 0.0 copy-start.1
  18.1 13.8 %all-to-all-start = ((bf16[64,2,6,128,128]{4,3,2,1,0:T(8,128)(2,1)}), bf16[64,2,6,128,128]{4,3,2,1,0:T(8,128)(2,1)}, u32[]{:S(2)}, u32[]{:S(2)}) async-start(bf16[64,2,6,128,128]{4,3,2,1,0:T(8,128)(2,1)} %stack.11), calls=%async_computation | async-start | bytes 50331648 | tf_op jit(solution)/shard_map/all_to_all | solution.py:37
  31.9 0.0 reduce-scatter.2.cloned.1.call-start
  32.0 0.0 copy-done
  32.0 0.2 copy.24
  32.2 0.0 copy-done.1
  32.2 0.1 select_reduce_fusion.1
  32.3 0.2 select_reduce_fusion
  32.5 2.6 fusion.12
  35.7 581.8 %all-to-all-done = bf16[64,2,6,128,128]{4,3,2,1,0:T(8,128)(2,1)} async-done(((bf16[64,2,6,128,128]{4,3,2,1,0:T(8,128)(2,1)}), bf16[64,2,6,128,128]{4,3,2,1,0:T(8,128)(2,1)}, u32[]{:S(2)}, u32[]{:S(2)}) %all-to-all-start) | async-done | bytes 25165856 | tf_op jit(solution)/shard_map/all_to_all | solution.py:37
  617.5 59.6 %conditional.1 = (f32[6,128]{1,0:T(8,128)S(1)}, f32[6,128,128]{1,2,0:T(8,128)S(1)}) conditional(s32[]{:T(128)} %convert_element_type.12, () %tuple.13, (pred[128,8192]{1,0:T(8,128)(4,1)S(1)}, bf16[2,6,64,128,128]{4,3,1,0,2:T(8,128)(2,1)}, bf16[6,128,128]{1,2,0:T(8,128)(2,1)S(1)}) %tuple.28), branch_computations={%region_3.4_spmd, %region_4.7_spmd} | conditional | flops 3303013632 | bytes 154748944 | solution.py:71
  617.5 17.8 %fusion.14 = (bf16[1,6,64,128,128]{4,3,2,1,0:T(8,128)(2,1)}, bf16[1,6,64,128,128]{4,3,2,1,0:T(8,128)(2,1)}) fusion(bf16[2,6,64,128,128]{4,3,1,0,2:T(8,128)(2,1)} %get-tuple-element.26), kind=kLoop, calls=%fused_computation.30 | loop fusion | bytes 50331648 | tf_op jit(solution)/shard_map/cond/branch_1_fun/slice | solution.py:50
  635.3 13.6 %fusion = (f32[6,128]{1,0:T(8,128)S(1)}, f32[6,128,8192]{2,1,0:T(8,128)}) fusion(pred[128,8192]{1,0:T(8,128)(4,1)S(1)} %get-tuple-element.12, bf16[6,128,128]{1,2,0:T(8,128)(2,1)S(1)} %get-tuple-element.27, bf16[6,8192,128]{2,1,0:T(8,128)(2,1)} %bitcast.24), kind=kOutput, calls=%fused_computation.2 | convolution fusion | flops 1629486336 | bytes 38996992 | tf_op jit(solution)/shard_map/cond/branch_1_fun/hqd,hkd->hqk/dot_general | solution.py:52
  648.9 15.8 %fusion.3 = f32[6,128,128]{1,2,0:T(8,128)S(1)} fusion(bf16[6,8192,128]{2,1,0:T(8,128)(2,1)} %bitcast.25, f32[6,128,8192]{2,1,0:T(8,128)} %get-tuple-element.34, f32[6,128]{1,0:T(8,128)S(1)} %broadcast_maximum_fusion, pred[128,8192]{1,0:T(8,128)(4,1)S(1)} %get-tuple-element.12), kind=kOutput, calls=%fused_computation.5 | convolution fusion | flops 1642070016 | bytes 39193600 | tf_op jit(solution)/shard_map/cond | solution.py:71
  664.7 12.5 %fusion.2 = f32[6,128]{1,0:T(8,128)S(1)} fusion(f32[6,128,8192]{2,1,0:T(8,128)} %get-tuple-element.34, f32[6,128]{1,0:T(8,128)S(1)} %broadcast_maximum_fusion, pred[128,8192]{1,0:T(8,128)(4,1)S(1)} %get-tuple-element.12), kind=kLoop, calls=%fused_computation.4 | loop fusion | flops 31456512 | bytes 26220544 | tf_op jit(solution)/shard_map/cond/branch_1_fun/reduce_sum | solution.py:58
  677.2 4.8 convolution_convert_fusion
  682.0 0.0 reduce-scatter.2.cloned.1.call-update
  682.0 67.0 %reduce-scatter.2.cloned.1.call-done = bf16[128,1024]{1,0:T(8,128)(2,1)} async-done(((bf16[128,4096]{1,0:T(8,128)(2,1)}), bf16[128,1024]{1,0:T(8,128)(2,1)}) %reduce-scatter.2.cloned.1.call-update) | async-done | bytes 262160 | tf_op jit(solution)/shard_map/reduce_scatter | solution.py:76
  (9 shorter events, 0.1 us)
Async XLA Ops:
  18.1 13.9 %copy-start = (bf16[128,768]{1,0:T(8,128)(2,1)S(1)}, bf16[128,768]{1,0:T(8,128)(2,1)}, u32[]{:S(2)}) copy-start(bf16[128,768]{1,0:T(8,128)(2,1)} %param.7) | copy-start | bytes 589828
  18.1 14.1 %copy-start.1 = (s32[3]{0:T(128)S(1)}, s32[3]{0:T(128)}, u32[]{:S(2)}) copy-start(s32[3]{0:T(128)} %param.11) | copy-start | bytes 40
  18.1 599.5 %all-to-all-start = ((bf16[64,2,6,128,128]{4,3,2,1,0:T(8,128)(2,1)}), bf16[64,2,6,128,128]{4,3,2,1,0:T(8,128)(2,1)}, u32[]{:S(2)}, u32[]{:S(2)}) async-start(bf16[64,2,6,128,128]{4,3,2,1,0:T(8,128)(2,1)} %stack.11), calls=%async_computation | async-start | bytes 50331648 | tf_op jit(solution)/shard_map/all_to_all | solution.py:37
  31.9 717.1 %reduce-scatter.2.cloned.1.call-start = ((), (), s32[]{:S(2)}) async-start(), calls=%async_computation.2 | async-start | bytes 1310720 | tf_op jit(solution)/shard_map/reduce_scatter | solution.py:76
Sparse Core Ops, SparseCore 0:
  682.1 66.8 reduce-scatter.1
